TPU v7x, 128 devices: a whole 4x4x4 slice. The times are simulated.
128 devices in a mesh: blk: 2 (over core), smp: 64 (over z, y, x).
Axes of the slice: x: 4, y: 4, z: 4, core: 2. Of those that a mesh axis runs over, the one named last changes fastest.
Arguments:
- genotypes: bfloat16 [2, 65536, 2048], P('blk', 'smp'), may hold values from -2 to 10, as said below
- sizes: int32 [2], P('blk'), may hold values from 1024 to 2048, as said below
- start: float32 [2, 2048, 256], P('blk', 'smp'), may hold values from -6 to 6
Outputs:
- basis: float32 [2, 2048, 256], P('blk', 'smp')
- scaled: float32 [2, 256, 256], P('blk')
Inputs may be any that keep to these rules, and one draw needn't show every extreme that they name: `sizes`: at least one block has exactly 2048 SNPs. `genotypes`: each column is a standardized count of 0, 1 or 2 alleles; columns at or past a block's size hold values that the block does not use.
All inputs are finite; a program needn't handle non-finite values.
Results may differ from a plain program's by a relative error of at most 0.0003.
Values may be sent and summed in bfloat16 or wider, within the bound.
A program may use at most 128 MiB of HBM per device.

v0:
```python
import math

import jax
import jax.numpy as jnp
from jax import lax
from jax.sharding import PartitionSpec as P

CAP = 2048
K = 256
ITERS = 2


def column_inner(left, right):
    return lax.dot_general(
        left,
        right,
        (((0,), (0,)), ((), ())),
        precision=lax.Precision.HIGHEST,
        preferred_element_type=jnp.float32,
    )


def form_gram(masked, samples_total):
    product = lax.dot_general(
        masked, masked, (((0,), (0,)), ((), ())), preferred_element_type=jnp.float32
    )
    return lax.psum_scatter(product / samples_total, "smp", scatter_dimension=0, tiled=True)


def apply_gram(gram, vectors):
    return jnp.dot(
        gram,
        lax.all_gather(vectors, "smp", axis=0, tiled=True),
        precision=lax.Precision.HIGHEST,
        preferred_element_type=jnp.float32,
    )


def orthonormal(image):
    inner = lax.psum(column_inner(image, image), "smp")
    lower = jnp.linalg.cholesky(inner)
    return lax.linalg.triangular_solve(lower, image, left_side=False, lower=True, transpose_a=True)


def iterate(gram, vectors):
    for repeat in range(ITERS):
        vectors = orthonormal(apply_gram(gram, vectors))
    rayleigh = lax.psum(column_inner(vectors, apply_gram(gram, vectors)), "smp")
    return (vectors, rayleigh)


def body(genotypes, sizes, start):
    groups = lax.axis_size("smp")
    samples_total = genotypes.shape[1] * groups
    live = (lax.iota(jnp.int32, CAP) < sizes[0]).astype(jnp.bfloat16)
    masked = genotypes[0] * live[None, :]
    gram = form_gram(masked, samples_total)
    vectors, rayleigh = iterate(gram, start[0])
    bases = [vectors]
    projected = [rayleigh]
    stacked = jnp.stack(projected)
    partial_trace = jnp.sum(jnp.trace(stacked, axis1=1, axis2=2))
    total = lax.psum(partial_trace, "blk")
    blocks_all = genotypes.shape[0] * lax.axis_size("blk")
    scaled = stacked * (blocks_all * K) / total
    basis = jnp.stack(bases) * math.sqrt(CAP)
    return (basis, scaled)


def solution(mesh):
    return jax.shard_map(
        body,
        mesh=mesh,
        in_specs=(P("blk", "smp", None), P("blk"), P("blk", "smp", None)),
        out_specs=(P("blk", "smp", None), P("blk", None, None)),
        check_vma=False,
    )
```

profile of v0, /device:TPU:1, one launch (start us, length us, event | category | flops | bytes accessed | tf_op | source)
XLA Modules:
  0.0 1123.9 jit_solution(2824407111754763374)
XLA Ops:
  7.2 0.7 all-gather.9.cloned.1.call-update
  8.6 15.2 %convolution_multiply_fusion = f32[2048,2048]{1,0:T(8,128)} fusion(bf16[1,1024,2048]{2,1,0:T(8,128)(2,1)} %param.6, bf16[2048]{0:T(1024)(128)(2,1)S(1)} %fusion.25), kind=kOutput, calls=%fused_computation.4 | convolution fusion | flops 8596226048 | bytes 20975616 | tf_op jit(solution)/shard_map/dot_general | solution.py:24
  23.9 53.9 %all-gather.9.cloned.1.call-done = f32[1,2048,256]{2,1,0:T(8,128)} async-done(((f32[1,32,256]{2,1,0:T(8,128)}), f32[1,2048,256]{2,1,0:T(8,128)}) %all-gather.9.cloned.1.call-update) | async-done | bytes 2097168 | tf_op jit(solution)/shard_map/all_gather | solution.py:33
  77.8 345.8 %reduce-scatter.2.cloned.1.call-done = f32[32,2048]{1,0:T(8,128)} async-done(((f32[2048,2048]{1,0:T(8,128)}), f32[32,2048]{1,0:T(8,128)}) %reduce-scatter.2.cloned.1.call-update) | async-done | bytes 262160 | tf_op jit(solution)/shard_map/reduce_scatter | solution.py:27
  423.6 2.8 fusion.2
  426.4 1.1 fusion.29
  427.5 0.2 all-gather.5.cloned.1.call-start
  427.8 168.1 %all-reduce.5.cloned.1.call-done = f32[256,256]{0,1:T(8,128)} async-done(((f32[256,256]{0,1:T(8,128)}), f32[256,256]{0,1:T(8,128)}) %all-reduce.5.cloned.1.call-update) | async-done | bytes 262160 | tf_op jit(solution)/shard_map/psum | solution.py:40
  595.8 1.1 copy.6
  596.9 1.0 fusion.6
  598.0 11.7 %cholesky.130 = f32[128,128]{1,0:T(8,128)S(1)} custom-call(f32[128,128]{1,0:T(8,128)S(1)} %cholesky.194), custom_call_target="Cholesky" | custom-call | tf_op jit(solution)/shard_map/jit(cholesky)/cholesky | solution.py:41
  609.7 9.8 custom-call.13
  619.8 0.3 convolution_subtract_fusion.1
  620.1 11.7 %cholesky.147 = f32[128,128]{1,0:T(8,128)S(1)} custom-call(f32[128,128]{1,0:T(8,128)S(1)} %convolution_subtract_fusion.1), custom_call_target="Cholesky" | custom-call | tf_op jit(solution)/shard_map/jit(cholesky)/cholesky | solution.py:41
  631.8 0.7 compare_reduce_fusion.2
  634.0 4.3 while.4
  634.2 0.6 fusion.53
  634.8 1.4 bitcast_dynamic-update-slice_fusion.4
  636.3 0.6 fusion.53
  636.9 1.4 bitcast_dynamic-update-slice_fusion.4
  638.3 19.7 %custom-call.14 = f32[2,128,128]{1,2,0:T(8,128)S(1)} custom-call(f32[2,128,128]{2,1,0:T(8,128)S(1)} %get-tuple-element.18), custom_call_target="InvertDiagBlocksLowerTriangular" | custom-call | tf_op jit(solution)/shard_map/triangular_solve/custom-call.0 | solution.py:42
  658.6 0.6 pad_maximum_fusion
  659.3 63.2 %all-gather.5.cloned.1.call-done = f32[2048,256]{1,0:T(8,128)} async-done(((f32[32,256]{1,0:T(8,128)}), f32[2048,256]{1,0:T(8,128)}) %all-gather.5.cloned.1.call-update) | async-done | bytes 2097168 | tf_op jit(solution)/shard_map/all_gather | solution.py:33
  722.5 2.7 fusion.30
  725.1 1.1 fusion.31
  726.3 125.2 %all-reduce.7.cloned.1.call-done = f32[256,256]{0,1:T(8,128)} async-done(((f32[256,256]{0,1:T(8,128)}), f32[256,256]{0,1:T(8,128)}) %all-reduce.7.cloned.1.call-update) | async-done | bytes 262160 | tf_op jit(solution)/shard_map/psum | solution.py:40
  851.6 1.1 copy.8
  852.7 1.0 fusion.5
  853.7 11.7 %cholesky.164 = f32[128,128]{1,0:T(8,128)S(1)} custom-call(f32[128,128]{1,0:T(8,128)S(1)} %cholesky.197), custom_call_target="Cholesky" | custom-call | tf_op jit(solution)/shard_map/jit(cholesky)/cholesky | solution.py:41
  865.4 9.8 custom-call.15
  875.5 0.3 convolution_subtract_fusion
  875.7 11.7 %cholesky.181 = f32[128,128]{1,0:T(8,128)S(1)} custom-call(f32[128,128]{1,0:T(8,128)S(1)} %convolution_subtract_fusion), custom_call_target="Cholesky" | custom-call | tf_op jit(solution)/shard_map/jit(cholesky)/cholesky | solution.py:41
  887.5 0.6 compare_reduce_fusion
  888.1 0.6 compare_reduce_fusion.1
  890.1 4.3 while.5
  890.4 0.6 fusion.54
  891.0 1.4 bitcast_dynamic-update-slice_fusion.5
  892.4 0.6 fusion.54
  893.0 1.4 bitcast_dynamic-update-slice_fusion.5
  894.4 19.7 %custom-call.16 = f32[2,128,128]{1,2,0:T(8,128)S(1)} custom-call(f32[2,128,128]{2,1,0:T(8,128)S(1)} %get-tuple-element.19), custom_call_target="InvertDiagBlocksLowerTriangular" | custom-call | tf_op jit(solution)/shard_map/triangular_solve/custom-call.0 | solution.py:42
  914.6 0.6 pad_maximum_fusion.1
  915.4 63.2 %all-gather.7.cloned.1.call-done = f32[2048,256]{1,0:T(8,128)} async-done(((f32[32,256]{1,0:T(8,128)}), f32[2048,256]{1,0:T(8,128)}) %all-gather.7.cloned.1.call-update) | async-done | bytes 2097168 | tf_op jit(solution)/shard_map/all_gather | solution.py:33
  978.5 2.7 fusion.32
  981.2 1.1 fusion.26
  982.3 125.4 %all-reduce.9.cloned.1.call-done = f32[256,256]{1,0:T(8,128)} async-done(((f32[256,256]{1,0:T(8,128)}), f32[256,256]{1,0:T(8,128)}) %all-reduce.9.cloned.1.call-update) | async-done | bytes 262160 | tf_op jit(solution)/shard_map/psum | solution.py:48
  1107.8 1.6 select_reduce_fusion
  1109.4 5.4 psum.31
  1114.8 2.3 divide_bitcast_fusion
  (41 shorter events, 2.2 us)
Async XLA Ops:
  7.2 70.6 %all-gather.9.cloned.1.call-start = ((), (), s32[]{:S(2)}) async-start(), calls=%async_computation.7 | async-start | bytes 2129920 | tf_op jit(solution)/shard_map/all_gather | solution.py:33
  7.9 415.7 %reduce-scatter.2.cloned.1.call-start = ((), (), s32[]{:S(2)}) async-start(), calls=%async_computation.1 | async-start | bytes 17039360 | tf_op jit(solution)/shard_map/reduce_scatter | solution.py:27
  23.8 572.0 %all-reduce.5.cloned.1.call-start = ((), (), s32[]{:S(2)}) async-start(), calls=%async_computation.2 | async-start | bytes 524288 | tf_op jit(solution)/shard_map/psum | solution.py:40
  427.5 294.9 %all-gather.5.cloned.1.call-start = ((), (), s32[]{:S(2)}) async-start(), calls=%async_computation.3 | async-start | bytes 2129920 | tf_op jit(solution)/shard_map/all_gather | solution.py:33
  596.9 125.5 %copy-start = (f32[32,2048]{1,0:T(8,128)S(1)}, f32[32,2048]{1,0:T(8,128)}, u32[]{:S(2)}) copy-start(f32[32,2048]{1,0:T(8,128)} %reduce-scatter.2.cloned.1.call-done) | copy-start | bytes 786436
  659.2 192.3 %all-reduce.7.cloned.1.call-start = ((), (), s32[]{:S(2)}) async-start(), calls=%async_computation.4 | async-start | bytes 524288 | tf_op jit(solution)/shard_map/psum | solution.py:40
  726.3 252.2 %all-gather.7.cloned.1.call-start = ((), (), s32[]{:S(2)}) async-start(), calls=%async_computation.5 | async-start | bytes 2129920 | tf_op jit(solution)/shard_map/all_gather | solution.py:33
  915.3 192.5 %all-reduce.9.cloned.1.call-start = ((), (), s32[]{:S(2)}) async-start(), calls=%async_computation.6 | async-start | bytes 524288 | tf_op jit(solution)/shard_map/psum | solution.py:48
Sparse Core Ops, SparseCore 0:
  10.8 66.8 all-gather.8
  80.2 343.3 reduce-scatter.1
  428.9 166.8 all-reduce.4
  659.4 63.0 all-gather.4
  727.6 123.9 all-reduce.6
  915.4 63.0 all-gather.6
  983.8 123.9 all-reduce.8
where the time goes:
time: 1120 us
  waiting for transfers between devices  946 us (84%)
  other arithmetic  115 us (10%)
  matrix products  28.7 us (3%)
  between operations  17.7 us (2%)
    reduce_scatter x1, waiting for transfers between devices, form_gram(): lax.psum_scatter(product / samples_total, 'smp', scatter_dimension=0, til...  346 us
    psum x2, waiting for transfers between devices, orthonormal(): inner = lax.psum(column_inner(image, image), 'smp')  293 us
    all_gather x3, waiting for transfers between devices, apply_gram(): lax.all_gather(vectors, 'smp', axis=0, tiled=True)  180 us
    psum x1, waiting for transfers between devices, iterate(): rayleigh = lax.psum(column_inner(vectors, apply_gram(gram, vectors)), 'smp')  125 us
    another operation x13, other arithmetic, orthonormal(): lower = jnp.linalg.cholesky(inner)  68.6 us
    another operation x7, other arithmetic, orthonormal(): lax.linalg.triangular_solve(lower, image, left_side=False, lower=True, tr...  40.7 us
  transfers between devices with their start and end apart: 7, of which 7 were waited for; matrix products, arithmetic and copies ran while one was open for 1% of the time, Pallas kernels for 0%

commit v1 on v0

v1 whole, which is shorter than its diff:
```python
import functools
import math

import jax
import jax.numpy as jnp
from jax import lax
from jax.experimental import pallas as pl
from jax.experimental.pallas import tpu as pltpu
from jax.sharding import PartitionSpec as P

CAP = 2048
K = 256
F32 = jnp.float32
BF16 = jnp.bfloat16
MESH = pl.DeviceIdType.MESH
ORDERS = ((0, 1, 2), (1, 2, 0), (2, 0, 1))
SUM_ROWS = ((0, 24), (24, 24), (48, 16))
GATHER_ROWS = ((0, 48), (48, 48), (96, 32))


def split3(v):
    high = v.astype(BF16).astype(F32)
    rest = v - high
    middle = rest.astype(BF16).astype(F32)
    return high, middle, rest - middle


def exact(a, b, dims):
    return lax.dot_general(
        a, b, (dims, ((), ())), precision=lax.Precision.HIGHEST, preferred_element_type=F32
    )


def factor8(block):
    sub = lax.broadcasted_iota(jnp.int32, (8, 128), 0)
    a = {}
    for s in range(8):
        column = jnp.broadcast_to(block[:, s : s + 1], (8, 128))
        for t in range(s, 8):
            a[t, s] = jnp.broadcast_to(column[t : t + 1, :], (8, 128))
    inv = []
    for s in range(8):
        r = lax.rsqrt(a[s, s])
        inv.append(r)
        for t in range(s + 1, 8):
            a[t, s] = a[t, s] * r
        for t in range(s + 1, 8):
            for u in range(s + 1, t + 1):
                a[t, u] = a[t, u] - a[t, s] * a[u, s]
    w = {}
    for s in range(8):
        w[s, s] = inv[s]
        for t in range(s + 1, 8):
            acc = a[t, s] * w[s, s]
            for u in range(s + 1, t):
                acc = acc + a[t, u] * w[u, s]
            w[t, s] = -acc * inv[t]
    columns = []
    for s in range(8):
        col = jnp.where(sub == s, w[s, s], 0.0)
        for t in range(s + 1, 8):
            col = jnp.where(sub == t, w[t, s], col)
        columns.append(col)
    return columns


def factor_group(aug, half, g):
    first = half * 128
    row = pl.multiple_of(first + g * 8, 8)
    panel = aug[pl.ds(row, 8), :]
    block = pltpu.roll(panel[:, first : first + 128], lax.rem(128 - g * 8, 128), 1)
    columns = factor8(block)
    u = None
    for s in range(8):
        term = jnp.concatenate([columns[s]] * 4, axis=1) * jnp.broadcast_to(panel[s : s + 1, :], (8, 512))
        u = term if u is None else u + term
    aug[pl.ds(row, 8), :] = u
    left = u[:, first:256]
    lane = lax.broadcasted_iota(jnp.int32, left.shape, 1) + first
    left = jnp.where(lane > row + 7, left, 0.0)
    lh, lm, ll = split3(left)
    uh, um, ul = split3(u)
    lhs = jnp.concatenate([lh, lh, lm, lm, lh, ll], axis=0).astype(BF16)
    rhs = jnp.concatenate([uh, um, uh, um, ul, uh], axis=0).astype(BF16)
    update = lax.dot_general(lhs, rhs, (((0,), (0,)), ((), ())), preferred_element_type=F32)
    aug[first:256, :] = aug[first:256, :] - update


def factor_start(aug, inner):
    aug[:, 0:256] = inner
    r = lax.broadcasted_iota(jnp.int32, (256, 256), 0)
    c = lax.broadcasted_iota(jnp.int32, (256, 256), 1)
    aug[:, 256:512] = jnp.where(r == c, 1.0, 0.0).astype(F32)


def factor_quarter(aug, quarter):
    @pl.loop(8 * (quarter % 2), 8 * (quarter % 2) + 8)
    def _(g):
        factor_group(aug, quarter // 2, g)


def symmetric(high, low):
    tall = (((0,), (0,)), ((), ()))
    first = lax.dot_general(high, jnp.concatenate([high, low], axis=1), tall, preferred_element_type=F32)
    last = lax.dot_general(low, low, tall, preferred_element_type=F32)
    return first, last


def kernel(sizes, start, x_hbm, basis, scaled, x, xt, gath, y, part, sum1, sum2, got1, got2, got3, aug, inner,
           mine, mgot1, mgot2, mgot3, mall, tbuf, xsem, gs, gr, ss, sr, ms, mr, ts, tr):
    blk = lax.axis_index("blk")
    smp = lax.axis_index("smp")
    at = [smp // 16, lax.rem(smp // 4, 4), lax.rem(smp, 4)]

    def peer(axis, pos):
        where = list(at)
        where[axis] = pos
        return (blk, where[0] * 16 + where[1] * 4 + where[2])

    load = pltpu.make_async_copy(x_hbm, x, xsem)
    load.start()
    barrier = pltpu.get_barrier_semaphore()
    for axis in range(3):
        for d in (1, 2, 3):
            pl.semaphore_signal(barrier, inc=1, device_id=peer(axis, lax.rem(at[axis] + d, 4)), device_id_type=MESH)
    pl.semaphore_signal(barrier, inc=1, device_id=(1 - blk, smp), device_id_type=MESH)

    size = sizes[0]
    live = lax.broadcasted_iota(jnp.int32, (32, 256), 0) + smp * 32 < size

    def put_own(buf, rows):
        high = rows.astype(BF16)
        low = (rows - high.astype(F32)).astype(BF16)
        for i, v in enumerate((high[:, :128], high[:, 128:], low[:, :128], low[:, 128:])):
            buf[at[0], at[1], at[2], 32 * i : 32 * i + 32, :] = v

    put_own(gath.at[0], jnp.where(live, start[0], 0.0))
    pl.semaphore_wait(barrier, 10)

    def copies(src, dst, send, recv, axis):
        out = []
        for d in (1, 2, 3):
            pos = lax.rem(at[axis] + d, 4)
            c = pltpu.make_async_remote_copy(
                src_ref=src(pos), dst_ref=dst(d), send_sem=send.at[d - 1], recv_sem=recv.at[d - 1],
                device_id=peer(axis, pos), device_id_type=MESH,
            )
            c.start()
            out.append(c)
        return out

    def gather(phase):
        buf = gath.at[phase % 2]
        for stage in range(3):
            running = []
            for c, order in enumerate(ORDERS):
                r0, n = GATHER_ROWS[c]
                known = order[:stage]
                idx = tuple(slice(None) if a in known else at[a] for a in range(3)) + (pl.ds(r0, n),)
                view = buf.at[idx]
                running.append(copies(lambda pos: view, lambda d: view, gs.at[phase, c, stage], gr.at[phase, c, stage], order[stage]))
            yield
            for cs in running:
                for k in cs:
                    k.wait()

    def halves(buf):
        full = buf[...]
        p = [full[:, :, :, 32 * i : 32 * i + 32, :].reshape(CAP, 128) for i in range(4)]
        return jnp.concatenate(p[:2], axis=1), jnp.concatenate(p[2:], axis=1)

    def project(phase):
        @pl.loop(0, 4)
        def _(m):
            rows = pl.ds(pl.multiple_of(m * 256, 256), 256)
            high, low = halves(gath.at[phase])
            t = jnp.dot(x[rows, :], high, preferred_element_type=F32) + jnp.dot(x[rows, :], low, preferred_element_type=F32)
            th = t.astype(BF16)
            y[rows, 0:256] = th
            y[rows, 256:512] = (t - th.astype(F32)).astype(BF16)

    def expand():
        @pl.loop(0, 8)
        def _(m):
            rows = pl.ds(pl.multiple_of(m * 256, 256), 256)
            t = jnp.dot(xt[rows, :], y[:, 0:256], preferred_element_type=F32)
            t = t + jnp.dot(xt[rows, :], y[:, 256:512], preferred_element_type=F32)
            y0 = 2 * lax.rem(m, 2)
            part[m // 2, pl.ds(y0, 2), :, 0:32, :] = t[:, :128].reshape(2, 4, 32, 128)
            part[m // 2, pl.ds(y0, 2), :, 32:64, :] = t[:, 128:].reshape(2, 4, 32, 128)

    def pick(axis_index, n, pos):
        return tuple(pos if i == axis_index else slice(None) for i in range(n))

    def scatter(phase, result):
        running = []
        for c, (a1, a2, a3) in enumerate(ORDERS):
            rows = (pl.ds(*SUM_ROWS[c]),)
            running.append(copies(
                lambda pos: part.at[pick(a1, 3, pos) + rows], lambda d: got1.at[(d - 1, slice(None), slice(None)) + rows],
                ss.at[phase, c, 0], sr.at[phase, c, 0], a1))
        yield
        running2 = []
        for c, (a1, a2, a3) in enumerate(ORDERS):
            r0, n = SUM_ROWS[c]
            for k in running[c]:
                k.wait()
            v = part[pick(a1, 3, at[a1]) + (slice(r0, r0 + n),)]
            for d in range(3):
                v = v + got1[d, :, :, r0 : r0 + n, :]
            sum1[:, :, r0 : r0 + n, :] = v
            i2 = [a for a in range(3) if a != a1].index(a2)
            rows = (pl.ds(r0, n),)
            running2.append(copies(
                lambda pos: sum1.at[pick(i2, 2, pos) + rows], lambda d: got2.at[(d - 1, slice(None)) + rows],
                ss.at[phase, c, 1], sr.at[phase, c, 1], a2))
        yield
        running3 = []
        for c, (a1, a2, a3) in enumerate(ORDERS):
            r0, n = SUM_ROWS[c]
            for k in running2[c]:
                k.wait()
            i2 = [a for a in range(3) if a != a1].index(a2)
            v = sum1[pick(i2, 2, at[a2]) + (slice(r0, r0 + n),)]
            for d in range(3):
                v = v + got2[d, :, r0 : r0 + n, :]
            sum2[:, r0 : r0 + n, :] = v
            rows = pl.ds(r0, n)
            running3.append(copies(
                lambda pos: sum2.at[pos, rows], lambda d: got3.at[d - 1, rows],
                ss.at[phase, c, 2], sr.at[phase, c, 2], a3))
        yield
        pieces = []
        for c, (a1, a2, a3) in enumerate(ORDERS):
            r0, n = SUM_ROWS[c]
            for k in running3[c]:
                k.wait()
            v = sum2[at[a3], r0 : r0 + n, :]
            for d in range(3):
                v = v + got3[d, r0 : r0 + n, :]
            pieces.append(v)
        v = jnp.concatenate(pieces, axis=0)
        v = jnp.concatenate([v[:32], v[32:]], axis=1)
        result.append(jnp.where(live, v * (1.0 / (64 * 1024)), 0.0))

    def square(phase):
        high, low = halves(gath.at[phase])
        first, last = symmetric(high, low)
        cross = first[:, 256:512]
        return first[:, 0:256] + (cross + cross.T) + last

    def run(gen):
        for _ in gen:
            pass

    g = gather(0)
    next(g)
    load.wait()

    @pl.loop(0, 8)
    def _(m):
        cols = pl.ds(pl.multiple_of(m * 256, 256), 256)
        xt[cols, :] = x[:, cols].T

    run(g)
    project(0)
    expand()
    out = []
    run(scatter(0, out))
    put_own(gath.at[1], out[0])
    run(gather(1))
    project(1)
    expand()
    out = []
    s = scatter(1, out)
    next(s)
    factor_start(aug, square(1))
    factor_quarter(aug, 0)
    factor_quarter(aug, 1)
    next(s)
    factor_quarter(aug, 2)
    next(s)
    factor_quarter(aug, 3)
    run(s)
    image = exact(out[0], aug[:, 256:512], ((1,), (1,)))
    put_own(gath.at[0], image)
    run(gather(2))
    project(0)

    first, last = symmetric(y[:, 0:256], y[:, 256:512])
    cross = first[:, 256:512]
    total = (first[:, 0:256] + (cross + cross.T) + last) * (1.0 / (64 * 1024))
    for c, (r, q) in enumerate(((0, 0), (0, 128), (128, 128))):
        mine[c] = total[r : r + 128, q : q + 128].reshape(4, 32, 128)
    running = [copies(lambda pos: mine.at[c, pos], lambda d: mgot1.at[c, d - 1], ms.at[c, 0], mr.at[c, 0], o[0]) for c, o in enumerate(ORDERS)]
    factor_start(aug, square(0))
    factor_quarter(aug, 0)
    for stage, (had, now) in ((1, (None, mgot2)), (2, (mgot2, mgot3)), (3, (mgot3, mall))):
        after = []
        for c, o in enumerate(ORDERS):
            for k in running[c]:
                k.wait()
            if stage == 1:
                v = mine[c, at[o[0]]] + mgot1[c, 0] + mgot1[c, 1] + mgot1[c, 2]
            else:
                v = had[c, 0] + had[c, 1] + had[c, 2] + had[c, 3]
            axis = o[stage] if stage < 3 else o[0]
            now[c, at[axis]] = v
            view = now.at[c, at[axis]]
            after.append(copies(lambda pos: view, lambda d: view, ms.at[c, stage], mr.at[c, stage], axis))
        running = after
        factor_quarter(aug, stage)
    low = aug[:, 256:512]
    basis[0] = exact(image, low, ((1,), (1,))) * math.sqrt(CAP)
    for cs in running:
        for k in cs:
            k.wait()
    b00, b01, b11 = (mall[c].reshape(128, 128) for c in range(3))
    full = jnp.concatenate([jnp.concatenate([b00, b01], axis=1), jnp.concatenate([b01.T, b11], axis=1)], axis=0)
    ray = exact(exact(low, full, ((1,), (0,))), low, ((1,), (1,)))
    r = lax.broadcasted_iota(jnp.int32, (K, K), 0)
    q = lax.broadcasted_iota(jnp.int32, (K, K), 1)
    trace = jnp.sum(jnp.where(r == q, ray, 0.0), axis=(0, 1), keepdims=True)
    tbuf[0] = jnp.broadcast_to(trace, (8, 128))
    c = pltpu.make_async_remote_copy(
        src_ref=tbuf.at[0], dst_ref=tbuf.at[1], send_sem=ts, recv_sem=tr, device_id=(1 - blk, smp), device_id_type=MESH
    )
    c.start()
    c.wait()
    both = tbuf[0, 0:1, 0:1] + tbuf[1, 0:1, 0:1]
    scaled[0] = ray * (2.0 * K) / both


def body(genotypes, sizes, start):
    vm = pltpu.VMEM
    dma = pltpu.SemaphoreType.DMA
    return pl.pallas_call(
        kernel,
        out_shape=(jax.ShapeDtypeStruct((1, 32, K), F32), jax.ShapeDtypeStruct((1, K, K), F32)),
        in_specs=[
            pl.BlockSpec(memory_space=pltpu.SMEM),
            pl.BlockSpec(memory_space=pltpu.VMEM),
            pl.BlockSpec(memory_space=pl.ANY),
        ],
        out_specs=(pl.BlockSpec(memory_space=pltpu.VMEM), pl.BlockSpec(memory_space=pltpu.VMEM)),
        scratch_shapes=[
            vm((1024, CAP), BF16),
            vm((CAP, 1024), BF16),
            vm((2, 4, 4, 4, 128, 128), BF16),
            vm((1024, 512), BF16),
            vm((4, 4, 4, 64, 128), F32),
            vm((4, 4, 64, 128), F32),
            vm((4, 64, 128), F32),
            vm((3, 4, 4, 64, 128), F32),
            vm((3, 4, 64, 128), F32),
            vm((3, 64, 128), F32),
            vm((K, 2 * K), F32),
            vm((K, K), F32),
            vm((3, 4, 32, 128), F32),
            vm((3, 3, 32, 128), F32),
            vm((3, 4, 32, 128), F32),
            vm((3, 4, 32, 128), F32),
            vm((3, 4, 32, 128), F32),
            vm((2, 8, 128), F32),
            dma,
            dma((3, 3, 3, 3)),
            dma((3, 3, 3, 3)),
            dma((2, 3, 3, 3)),
            dma((2, 3, 3, 3)),
            dma((3, 4, 3)),
            dma((3, 4, 3)),
            dma,
            dma,
        ],
        compiler_params=pltpu.CompilerParams(
            collective_id=0, has_side_effects=True, vmem_limit_bytes=60 * 2**20
        ),
    )(sizes, start, genotypes.reshape(genotypes.shape[1:]))


def solution(mesh):
    return jax.shard_map(
        body,
        mesh=mesh,
        in_specs=(P("blk", "smp", None), P("blk"), P("blk", "smp", None)),
        out_specs=(P("blk", "smp", None), P("blk", None, None)),
        check_vma=False,
    )
```

time: 1120 us -> 142 us (0.13)
  waiting for transfers between devices: 946 us -> 0 us
  Pallas kernels: 0 us -> 138 us
  other arithmetic: 115 us -> 0 us
  matrix products: 28.7 us -> 0 us
  between operations: 17.7 us -> 1.28 us
    psum x3 -> x0, waiting for transfers between devices: 419 us -> none  [the longest x2 293 us: orthonormal(): inner = lax.psum(column_inner(image, image), 'smp')]
    reduce_scatter x1 -> x0, waiting for transfers between devices: 346 us -> none  [form_gram(): lax.psum_scatter(product / samples_total, 'smp', scatter_dimension=0, til...]
    all_gather x3 -> x0, waiting for transfers between devices: 180 us -> none  [apply_gram(): lax.all_gather(vectors, 'smp', axis=0, tiled=True)]
    pallas_call x0 -> x1, Pallas kernels: none -> 138 us  [body(): pl.pallas_call(kernel, out_shape=(jax.ShapeDtypeStruct((1, 32, K), F32),...]
    another operation x20 -> x0, other arithmetic: 109 us -> none  [the longest x13 68.6 us: orthonormal(): lower = jnp.linalg.cholesky(inner)]
    dot_general x7 -> x0, matrix products: 26.7 us -> none  [the longest x1 15.2 us: form_gram(): lax.dot_general(masked, masked, (((0,), (0,)), ((), ())), preferred_eleme...]
  transfers between devices with their start and end apart: 7 -> 0, of which waited for: 7 -> 0; matrix products, arithmetic and copies ran while one was open for 1% -> 0% of each run, Pallas kernels for 0% -> 0%
where the time goes in v1:
time: 142 us
  Pallas kernels  138 us (97%)
  local copies, waits for them, and re-layouts  3.04 us (2%)
    pallas_call x1, Pallas kernels, body(): pl.pallas_call(kernel, out_shape=(jax.ShapeDtypeStruct((1, 32, K), F32),...  138 us
    unnamed x2, local copies, waits for them, and re-layouts  3.04 us

profile of v1, /device:TPU:1, one launch (start us, length us, event | category | flops | bytes accessed | tf_op | source)
XLA Modules:
  0.0 142.0 jit_solution(4573039102346292745)
XLA Ops:
  1.3 137.7 %shard_map.50 = (f32[1,32,256]{2,1,0:T(8,128)}, f32[1,256,256]{2,1,0:T(8,128)}) custom-call(s32[1]{0:T(128)S(6)} %copy.7.sizes, f32[1,32,256]{2,1,0:T(8,128)} %start.1, bf16[1024,2048]{1,0:T(8,128)(2,1)} %bitcast.1), custom_call_target="tpu_custom_call" | custom-call | tf_op jit(solution)/shard_map/pallas_call | solution.py:337
  139.0 1.4 copy.8
  140.3 1.7 %copy.9 = f32[1,256,256]{2,1,0:T(8,128)} copy(f32[1,256,256]{2,1,0:T(8,128)} %get-tuple-element.5) | data formatting | bytes 524288

commit v2 on v1

v2 whole, which is shorter than its diff:
```python
import functools
import math

import jax
import jax.numpy as jnp
from jax import lax
from jax.experimental import pallas as pl
from jax.experimental.pallas import tpu as pltpu
from jax.sharding import PartitionSpec as P

CAP = 2048
K = 256
F32 = jnp.float32
BF16 = jnp.bfloat16
MESH = pl.DeviceIdType.MESH
OTHERS = ((1, 2), (0, 2), (0, 1))
ORDERS = ((0, 1, 2), (1, 2, 0), (2, 0, 1))
SUM_ROWS = ((0, 24), (24, 24), (48, 16))
GATHER_ROWS = ((0, 48), (48, 48), (96, 32))


def split3(v):
    high = v.astype(BF16).astype(F32)
    rest = v - high
    middle = rest.astype(BF16).astype(F32)
    return high, middle, rest - middle


def exact(a, b, dims):
    return lax.dot_general(
        a, b, (dims, ((), ())), precision=lax.Precision.HIGHEST, preferred_element_type=F32
    )


def spread(block, first):
    return [jnp.broadcast_to(block[:, first + s : first + s + 1], (8, 128)) for s in range(8)]


def row_of(v, t):
    return jnp.broadcast_to(v[t : t + 1, :], v.shape)


def total(terms):
    terms = list(terms)
    while len(terms) > 1:
        terms = [terms[i] + terms[i + 1] if i + 1 < len(terms) else terms[i] for i in range(0, len(terms), 2)]
    return terms[0]


def factor8(columns):
    a = {(t, s): row_of(columns[s], t) for s in range(8) for t in range(s, 8)}
    inv = []
    for s in range(8):
        r = lax.rsqrt(a[s, s])
        inv.append(r)
        for t in range(s + 1, 8):
            a[t, s] = a[t, s] * r
        for t in range(s + 1, 8):
            for u in range(s + 1, t + 1):
                a[t, u] = a[t, u] - a[t, s] * a[u, s]
    w = {}
    for s in range(8):
        w[s, s] = inv[s]
        for t in range(s + 1, 8):
            acc = a[t, s] * w[s, s]
            for u in range(s + 1, t):
                acc = acc + a[t, u] * w[u, s]
            w[t, s] = -acc * inv[t]
    return w


def stack_rows(w):
    sub = lax.broadcasted_iota(jnp.int32, (8, 128), 0)
    columns = []
    for s in range(8):
        col = jnp.where(sub == s, w[s, s], 0.0)
        for t in range(s + 1, 8):
            col = jnp.where(sub == t, w[t, s], col)
        columns.append(wide(col))
    return columns


def wide(col):
    return jnp.concatenate([col] * 3, axis=1)


def six(v, right):
    a, b, c = split3(v)
    return jnp.concatenate([a, b, a, b, c, a] if right else [a, a, b, b, a, c], axis=0).astype(BF16)


TALL = (((0,), (0,)), ((), ()))


def factor_pair(aug, half, g):
    f = half * 128
    row = pl.multiple_of(f + g * 16, 16)
    next_row = pl.multiple_of(row + 8, 8)
    p1 = aug[pl.ds(row, 8), f : f + 384]
    p2 = aug[pl.ds(next_row, 8), f : f + 384]
    shift = lax.rem(128 - g * 16, 128)
    b1 = pltpu.roll(p1[:, 0:128], shift, 1)
    b2 = pltpu.roll(p2[:, 0:128], shift, 1)
    w1 = factor8(spread(b1, 0))
    cross = spread(b2, 0)
    low = [total(cross[k] * w1[s, k] for k in range(s + 1)) for s in range(8)]
    back = [total(low[s] * w1[s, k] for s in range(k, 8)) for k in range(8)]
    b2 = b2 - total(back[k] * row_of(b1, k) for k in range(8))
    w2 = factor8(spread(b2, 8))
    c1 = stack_rows(w1)
    rows1 = [row_of(p1, k) for k in range(8)]
    u1 = total(c1[k] * rows1[k] for k in range(8))
    p2 = p2 - total(wide(back[k]) * rows1[k] for k in range(8))
    c2 = stack_rows(w2)
    u2 = total(c2[k] * row_of(p2, k) for k in range(8))
    aug[pl.ds(row, 8), f : f + 384] = u1
    aug[pl.ds(next_row, 8), f : f + 384] = u2
    u = jnp.concatenate([u1, u2], axis=0)
    left = u[:, 0:128]
    lane = lax.broadcasted_iota(jnp.int32, left.shape, 1)
    left = jnp.where(lane > g * 16 + 15, left, 0.0)
    update = lax.dot_general(six(left, False), six(u, True), TALL, preferred_element_type=F32)
    aug[f : f + 128, f : f + 384] = aug[f : f + 128, f : f + 384] - update


def factor_start(aug, inner):
    aug[:, 0:256] = inner
    r = lax.broadcasted_iota(jnp.int32, (256, 256), 0)
    c = lax.broadcasted_iota(jnp.int32, (256, 256), 1)
    aug[:, 256:512] = jnp.where(r == c, 1.0, 0.0).astype(F32)


def factor_part(aug, first, count):
    @pl.loop(first % 8, first % 8 + count)
    def _(g):
        factor_pair(aug, first // 8, g)

    if first + count == 8:
        aug[128:256, 128:384] = aug[128:256, 128:384] - exact(aug[0:128, 128:256], aug[0:128, 128:384], ((0,), (0,)))


def symmetric(high, low):
    tall = (((0,), (0,)), ((), ()))
    first = lax.dot_general(high, jnp.concatenate([high, low], axis=1), tall, preferred_element_type=F32)
    last = lax.dot_general(low, low, tall, preferred_element_type=F32)
    return first, last


def kernel(sizes, start, x_hbm, basis, scaled, x, xt, gath, y, part, sum1, got1, got2, aug,
           mine, mgot1, mgot2, mgot3, mall, tbuf, xsem, gs, gr, ls, lr, ms, mr, ts, tr):
    blk = lax.axis_index("blk")
    smp = lax.axis_index("smp")
    at = [smp // 16, lax.rem(smp // 4, 4), lax.rem(smp, 4)]

    def peer(axis, pos):
        where = list(at)
        where[axis] = pos
        return (blk, where[0] * 16 + where[1] * 4 + where[2])

    load = pltpu.make_async_copy(x_hbm, x, xsem)
    load.start()
    barrier = pltpu.get_barrier_semaphore()
    steps = [(dz, dy, dx) for dz in range(4) for dy in range(4) for dx in range(4) if 0 < (dz > 0) + (dy > 0) + (dx > 0) < 3]
    for step in steps:
        z, y_, x_ = (lax.rem(p + d, 4) for p, d in zip(at, step))
        pl.semaphore_signal(barrier, inc=1, device_id=(blk, z * 16 + y_ * 4 + x_), device_id_type=MESH)
    pl.semaphore_signal(barrier, inc=1, device_id=(1 - blk, smp), device_id_type=MESH)

    size = sizes[0]
    live = lax.broadcasted_iota(jnp.int32, (32, 256), 0) + smp * 32 < size

    def put_own(buf, rows):
        high = rows.astype(BF16)
        low = (rows - high.astype(F32)).astype(BF16)
        for i, v in enumerate((high[:, :128], high[:, 128:], low[:, :128], low[:, 128:])):
            buf[at[0], at[1], at[2], 32 * i : 32 * i + 32, :] = v

    put_own(gath.at[0], jnp.where(live, start[0], 0.0))
    pl.semaphore_wait(barrier, len(steps) + 1)

    def copies(src, dst, send, recv, axis):
        out = []
        for d in (1, 2, 3):
            pos = lax.rem(at[axis] + d, 4)
            c = pltpu.make_async_remote_copy(
                src_ref=src(pos), dst_ref=dst(d), send_sem=send.at[d - 1], recv_sem=recv.at[d - 1],
                device_id=peer(axis, pos), device_id_type=MESH,
            )
            c.start()
            out.append(c)
        return out

    def pick(axis_index, n, pos):
        return tuple(pos if i == axis_index else slice(None) for i in range(n))

    def place(c, pc, pu, rest=()):
        idx = [slice(None)] * 3
        idx[c], idx[OTHERS[c][0]] = pc, pu
        return tuple(idx) + rest

    def plane_copy(c, du, dv, src, dst, send, recv):
        u, v = OTHERS[c]
        where = list(at)
        where[u] = lax.rem(at[u] + du, 4)
        where[v] = lax.rem(at[v] + dv, 4)
        k = pltpu.make_async_remote_copy(
            src_ref=src, dst_ref=dst, send_sem=send.at[4 * du + dv - 1], recv_sem=recv.at[4 * du + dv - 1],
            device_id=(blk, where[0] * 16 + where[1] * 4 + where[2]), device_id_type=MESH,
        )
        k.start()
        return k

    def wait_all(running):
        for cs in running:
            for k in cs:
                k.wait()

    def gather(phase):
        buf = gath.at[phase % 2]
        short, long = {}, []
        for du in (2, 1, 3, 0):
            for c in range(3):
                view = buf.at[at[0], at[1], at[2], pl.ds(*GATHER_ROWS[c])]
                for dv in range(4):
                    if du + dv:
                        short[c, du, dv] = plane_copy(c, du, dv, view, view, gs.at[phase, c], gr.at[phase, c])
        yield
        for du in (0, 1, 3, 2):
            for c in range(3):
                for dv in range(4):
                    if du + dv:
                        short[c, du, dv].wait_recv()
                line = lax.rem(at[OTHERS[c][0]] + 4 - du, 4)
                view = buf.at[place(c, at[c], line, (pl.ds(*GATHER_ROWS[c]),))]
                long.append(copies(lambda pos: view, lambda d: view, ls.at[phase, c, du], lr.at[phase, c, du], c))
        for k in short.values():
            k.wait_send()
        wait_all(long)

    def halves(buf):
        full = buf[...]
        p = [full[:, :, :, 32 * i : 32 * i + 32, :].reshape(CAP, 128) for i in range(4)]
        return jnp.concatenate(p[:2], axis=1), jnp.concatenate(p[2:], axis=1)

    def project(phase):
        @pl.loop(0, 2)
        def _(m):
            rows = pl.ds(pl.multiple_of(m * 512, 512), 512)
            high, low = halves(gath.at[phase])
            t = jnp.dot(x[rows, :], high, preferred_element_type=F32) + jnp.dot(x[rows, :], low, preferred_element_type=F32)
            th = t.astype(BF16)
            y[rows, 0:256] = th
            y[rows, 256:512] = (t - th.astype(F32)).astype(BF16)

    def expand():
        @pl.loop(0, 4)
        def _(m):
            rows = pl.ds(pl.multiple_of(m * 512, 512), 512)
            t = jnp.dot(xt[rows, :], y[:, 0:256], preferred_element_type=F32)
            t = t + jnp.dot(xt[rows, :], y[:, 256:512], preferred_element_type=F32)
            part[m, :, :, 0:32, :] = t[:, :128].reshape(4, 4, 32, 128)
            part[m, :, :, 32:64, :] = t[:, 128:].reshape(4, 4, 32, 128)

    def scatter(phase, result):
        long, short = {}, {}
        for du in (2, 1, 3, 0):
            for c in range(3):
                rows = (pl.ds(*SUM_ROWS[c]),)
                line = lax.rem(at[OTHERS[c][0]] + du, 4)
                long[c, du] = copies(
                    lambda pos: part.at[place(c, pos, line, rows)], lambda d: got1.at[(d - 1, du, slice(None)) + rows],
                    ls.at[3 + phase, c, du], lr.at[3 + phase, c, du], c)
        yield
        for du in (2, 1, 3, 0):
            for c in range(3):
                r0, n = SUM_ROWS[c]
                for k in long[c, du]:
                    k.wait_recv()
                line = lax.rem(at[OTHERS[c][0]] + du, 4)
                v = part[place(c, at[c], line, (slice(r0, r0 + n),))]
                for d in range(3):
                    v = v + got1[d, du, :, r0 : r0 + n, :]
                sum1[du, :, r0 : r0 + n, :] = v
                for dv in range(4):
                    if du + dv:
                        pv = lax.rem(at[OTHERS[c][1]] + dv, 4)
                        short[c, du, dv] = plane_copy(
                            c, du, dv, sum1.at[du, pv, pl.ds(r0, n)], got2.at[4 * du + dv - 1, pl.ds(r0, n)],
                            gs.at[3 + phase, c], gr.at[3 + phase, c])
            yield
        for k in [k for ks in long.values() for k in ks]:
            k.wait_send()
        pieces = []
        for c in range(3):
            r0, n = SUM_ROWS[c]
            v = sum1[0, at[OTHERS[c][1]], r0 : r0 + n, :]
            for du in (2, 1, 3, 0):
                for dv in range(4):
                    if du + dv:
                        short[c, du, dv].wait()
                        v = v + got2[4 * du + dv - 1, r0 : r0 + n, :]
            pieces.append(v)
        v = jnp.concatenate(pieces, axis=0)
        v = jnp.concatenate([v[:32], v[32:]], axis=1)
        result.append(jnp.where(live, v * (1.0 / (64 * 1024)), 0.0))

    def square(phase):
        high, low = halves(gath.at[phase])
        first, last = symmetric(high, low)
        cross = first[:, 256:512]
        return first[:, 0:256] + (cross + cross.T) + last

    def run(gen):
        for _ in gen:
            pass

    g = gather(0)
    next(g)
    load.wait()

    @pl.loop(0, 8)
    def _(m):
        cols = pl.ds(pl.multiple_of(m * 256, 256), 256)
        xt[cols, :] = x[:, cols].T

    run(g)
    project(0)
    expand()
    out = []
    run(scatter(0, out))
    put_own(gath.at[1], out[0])
    run(gather(1))
    project(1)
    expand()
    out = []
    s = scatter(1, out)
    next(s)
    factor_start(aug, square(1))
    factor_part(aug, 0, 4)
    next(s)
    factor_part(aug, 4, 2)
    next(s)
    factor_part(aug, 6, 2)
    next(s)
    factor_part(aug, 8, 2)
    next(s)
    factor_part(aug, 10, 6)
    run(s)
    image = exact(out[0], aug[:, 256:512], ((1,), (1,)))
    put_own(gath.at[0], image)
    run(gather(2))
    project(0)

    first, last = symmetric(y[:, 0:256], y[:, 256:512])
    cross = first[:, 256:512]
    total = (first[:, 0:256] + (cross + cross.T) + last) * (1.0 / (64 * 1024))
    for c, (r, q) in enumerate(((0, 0), (0, 128), (128, 128))):
        mine[c] = total[r : r + 128, q : q + 128].reshape(4, 32, 128)
    running = [copies(lambda pos: mine.at[c, pos], lambda d: mgot1.at[c, d - 1], ms.at[c, 0], mr.at[c, 0], o[0]) for c, o in enumerate(ORDERS)]
    factor_start(aug, square(0))
    factor_part(aug, 0, 4)
    for stage, (had, now) in ((1, (None, mgot2)), (2, (mgot2, mgot3)), (3, (mgot3, mall))):
        after = []
        for c, o in enumerate(ORDERS):
            for k in running[c]:
                k.wait()
            if stage == 1:
                v = mine[c, at[o[0]]] + mgot1[c, 0] + mgot1[c, 1] + mgot1[c, 2]
            else:
                v = had[c, 0] + had[c, 1] + had[c, 2] + had[c, 3]
            axis = o[stage] if stage < 3 else o[0]
            now[c, at[axis]] = v
            view = now.at[c, at[axis]]
            after.append(copies(lambda pos: view, lambda d: view, ms.at[c, stage], mr.at[c, stage], axis))
        running = after
        factor_part(aug, 4 * stage, 4)
    low = aug[:, 256:512]
    basis[0] = exact(image, low, ((1,), (1,))) * math.sqrt(CAP)
    for cs in running:
        for k in cs:
            k.wait()
    b00, b01, b11 = (mall[c].reshape(128, 128) for c in range(3))
    full = jnp.concatenate([jnp.concatenate([b00, b01], axis=1), jnp.concatenate([b01.T, b11], axis=1)], axis=0)
    ray = exact(exact(low, full, ((1,), (0,))), low, ((1,), (1,)))
    r = lax.broadcasted_iota(jnp.int32, (K, K), 0)
    q = lax.broadcasted_iota(jnp.int32, (K, K), 1)
    trace = jnp.sum(jnp.where(r == q, ray, 0.0), axis=(0, 1), keepdims=True)
    tbuf[0] = jnp.broadcast_to(trace, (8, 128))
    c = pltpu.make_async_remote_copy(
        src_ref=tbuf.at[0], dst_ref=tbuf.at[1], send_sem=ts, recv_sem=tr, device_id=(1 - blk, smp), device_id_type=MESH
    )
    c.start()
    c.wait()
    both = tbuf[0, 0:1, 0:1] + tbuf[1, 0:1, 0:1]
    scaled[0] = ray * (2.0 * K) / both


def body(genotypes, sizes, start):
    vm = pltpu.VMEM
    dma = pltpu.SemaphoreType.DMA
    return pl.pallas_call(
        kernel,
        out_shape=(jax.ShapeDtypeStruct((1, 32, K), F32), jax.ShapeDtypeStruct((1, K, K), F32)),
        in_specs=[
            pl.BlockSpec(memory_space=pltpu.SMEM),
            pl.BlockSpec(memory_space=pltpu.VMEM),
            pl.BlockSpec(memory_space=pl.ANY),
        ],
        out_specs=(pl.BlockSpec(memory_space=pltpu.VMEM), pl.BlockSpec(memory_space=pltpu.VMEM)),
        scratch_shapes=[
            vm((1024, CAP), BF16),
            vm((CAP, 1024), BF16),
            vm((2, 4, 4, 4, 128, 128), BF16),
            vm((1024, 512), BF16),
            vm((4, 4, 4, 64, 128), F32),
            vm((4, 4, 64, 128), F32),
            vm((3, 4, 4, 64, 128), F32),
            vm((15, 64, 128), F32),
            vm((K, 2 * K), F32),
            vm((3, 4, 32, 128), F32),
            vm((3, 3, 32, 128), F32),
            vm((3, 4, 32, 128), F32),
            vm((3, 4, 32, 128), F32),
            vm((3, 4, 32, 128), F32),
            vm((2, 8, 128), F32),
            dma,
            dma((5, 3, 15)),
            dma((5, 3, 15)),
            dma((5, 3, 4, 3)),
            dma((5, 3, 4, 3)),
            dma((3, 4, 3)),
            dma((3, 4, 3)),
            dma,
            dma,
        ],
        compiler_params=pltpu.CompilerParams(
            collective_id=0, has_side_effects=True, vmem_limit_bytes=60 * 2**20
        ),
    )(sizes, start, genotypes.reshape(genotypes.shape[1:]))


def solution(mesh):
    return jax.shard_map(
        body,
        mesh=mesh,
        in_specs=(P("blk", "smp", None), P("blk"), P("blk", "smp", None)),
        out_specs=(P("blk", "smp", None), P("blk", None, None)),
        check_vma=False,
    )
```

time: 142 us -> 132 us (0.930)
  Pallas kernels: 138 us -> 127 us
    pallas_call x1, Pallas kernels: 138 us -> 127 us  [body(): pl.pallas_call(kernel, out_shape=(jax.ShapeDtypeStruct((1, 32, K), F32),...]
where the time goes in v2:
time: 132 us; the launch traced here: 131 us
  Pallas kernels  127 us (96%)
  local copies, waits for them, and re-layouts  3.04 us (2%)
    pallas_call x1, Pallas kernels, body(): pl.pallas_call(kernel, out_shape=(jax.ShapeDtypeStruct((1, 32, K), F32),...  127 us
    unnamed x2, local copies, waits for them, and re-layouts  3.04 us

profile of v2, /device:TPU:1, one launch (start us, length us, event | category | flops | bytes accessed | tf_op | source)
XLA Modules:
  0.0 131.5 jit_solution(5089922664151046437)
XLA Ops:
  1.3 127.2 %shard_map.50 = (f32[1,32,256]{2,1,0:T(8,128)}, f32[1,256,256]{2,1,0:T(8,128)}) custom-call(s32[1]{0:T(128)S(6)} %copy.7.sizes, f32[1,32,256]{2,1,0:T(8,128)} %start.1, bf16[1024,2048]{1,0:T(8,128)(2,1)} %bitcast.1), custom_call_target="tpu_custom_call" | custom-call | tf_op jit(solution)/shard_map/pallas_call | solution.py:401
  128.4 1.4 %copy.8 = f32[1,32,256]{2,1,0:T(8,128)} copy(f32[1,32,256]{2,1,0:T(8,128)} %get-tuple-element.4) | data formatting | bytes 65536
  129.8 1.7 %copy.9 = f32[1,256,256]{2,1,0:T(8,128)} copy(f32[1,256,256]{2,1,0:T(8,128)} %get-tuple-element.5) | data formatting | bytes 524288

commit v3 on v2

--- a/solution.py
+++ b/solution.py
@@ -178,9 +178,9 @@
     put_own(gath.at[0], jnp.where(live, start[0], 0.0))
     pl.semaphore_wait(barrier, len(steps) + 1)
 
-    def copies(src, dst, send, recv, axis):
+    def copies(src, dst, send, recv, axis, ds=(1, 2, 3)):
         out = []
-        for d in (1, 2, 3):
+        for d in ds:
             pos = lax.rem(at[axis] + d, 4)
             c = pltpu.make_async_remote_copy(
                 src_ref=src(pos), dst_ref=dst(d), send_sem=send.at[d - 1], recv_sem=recv.at[d - 1],
@@ -218,7 +218,7 @@
     def gather(phase):
         buf = gath.at[phase % 2]
         short, long = {}, []
-        for du in (2, 1, 3, 0):
+        for du in (0, 1, 3, 2):
             for c in range(3):
                 view = buf.at[at[0], at[1], at[2], pl.ds(*GATHER_ROWS[c])]
                 for dv in range(4):
@@ -252,24 +252,32 @@
             y[rows, 0:256] = th
             y[rows, 256:512] = (t - th.astype(F32)).astype(BF16)
 
-    def expand():
-        @pl.loop(0, 4)
+    def expand(z):
+        @pl.loop(0, 2)
         def _(m):
-            rows = pl.ds(pl.multiple_of(m * 512, 512), 512)
+            rows = pl.ds(pl.multiple_of(z * 512 + m * 256, 256), 256)
             t = jnp.dot(xt[rows, :], y[:, 0:256], preferred_element_type=F32)
             t = t + jnp.dot(xt[rows, :], y[:, 256:512], preferred_element_type=F32)
-            part[m, :, :, 0:32, :] = t[:, :128].reshape(4, 4, 32, 128)
-            part[m, :, :, 32:64, :] = t[:, 128:].reshape(4, 4, 32, 128)
+            part[z, pl.ds(2 * m, 2), :, 0:32, :] = t[:, :128].reshape(2, 4, 32, 128)
+            part[z, pl.ds(2 * m, 2), :, 32:64, :] = t[:, 128:].reshape(2, 4, 32, 128)
 
     def scatter(phase, result):
-        long, short = {}, {}
+        long, short = {(0, du): [] for du in range(4)}, {}
+
+        def send(c, du, d):
+            rows = (pl.ds(*SUM_ROWS[c]),)
+            line = lax.rem(at[OTHERS[c][0]] + du, 4)
+            long.setdefault((c, du), []).extend(copies(
+                lambda pos: part.at[place(c, pos, line, rows)], lambda d: got1.at[(d - 1, du, slice(None)) + rows],
+                ls.at[3 + phase, c, du], lr.at[3 + phase, c, du], c, d))
+
         for du in (2, 1, 3, 0):
-            for c in range(3):
-                rows = (pl.ds(*SUM_ROWS[c]),)
-                line = lax.rem(at[OTHERS[c][0]] + du, 4)
-                long[c, du] = copies(
-                    lambda pos: part.at[place(c, pos, line, rows)], lambda d: got1.at[(d - 1, du, slice(None)) + rows],
-                    ls.at[3 + phase, c, du], lr.at[3 + phase, c, du], c)
+            expand(lax.rem(at[0] + du, 4))
+            for c in (1, 2):
+                send(c, du, (1, 2, 3))
+            if du:
+                for line in (2, 1, 3, 0):
+                    send(0, line, (du,))
         yield
         for du in (2, 1, 3, 0):
             for c in range(3):
@@ -325,13 +333,11 @@
 
     run(g)
     project(0)
-    expand()
     out = []
     run(scatter(0, out))
     put_own(gath.at[1], out[0])
     run(gather(1))
     project(1)
-    expand()
     out = []
     s = scatter(1, out)
     next(s)
@@ -381,26 +387,30 @@
             k.wait()
     b00, b01, b11 = (mall[c].reshape(128, 128) for c in range(3))
     full = jnp.concatenate([jnp.concatenate([b00, b01], axis=1), jnp.concatenate([b01.T, b11], axis=1)], axis=0)
-    ray = exact(exact(low, full, ((1,), (0,))), low, ((1,), (1,)))
-    r = lax.broadcasted_iota(jnp.int32, (K, K), 0)
-    q = lax.broadcasted_iota(jnp.int32, (K, K), 1)
-    trace = jnp.sum(jnp.where(r == q, ray, 0.0), axis=(0, 1), keepdims=True)
-    tbuf[0] = jnp.broadcast_to(trace, (8, 128))
+    left = exact(low, full, ((1,), (0,)))
+    tbuf[0] = jnp.broadcast_to(jnp.sum(left * low, axis=(0, 1), keepdims=True), (8, 128))
     c = pltpu.make_async_remote_copy(
         src_ref=tbuf.at[0], dst_ref=tbuf.at[1], send_sem=ts, recv_sem=tr, device_id=(1 - blk, smp), device_id_type=MESH
     )
     c.start()
+    ray = exact(left, low, ((1,), (1,)))
     c.wait()
     both = tbuf[0, 0:1, 0:1] + tbuf[1, 0:1, 0:1]
     scaled[0] = ray * (2.0 * K) / both
 
 
+def hand_out(basis, scaled, basis_out, scaled_out):
+    basis_out[...] = basis[...]
+    scaled_out[...] = scaled[...]
+
+
 def body(genotypes, sizes, start):
     vm = pltpu.VMEM
     dma = pltpu.SemaphoreType.DMA
-    return pl.pallas_call(
+    shapes = (jax.ShapeDtypeStruct((1, 32, K), F32), jax.ShapeDtypeStruct((1, K, K), F32))
+    results = pl.pallas_call(
         kernel,
-        out_shape=(jax.ShapeDtypeStruct((1, 32, K), F32), jax.ShapeDtypeStruct((1, K, K), F32)),
+        out_shape=shapes,
         in_specs=[
             pl.BlockSpec(memory_space=pltpu.SMEM),
             pl.BlockSpec(memory_space=pltpu.VMEM),
@@ -437,6 +447,7 @@
             collective_id=0, has_side_effects=True, vmem_limit_bytes=60 * 2**20
         ),
     )(sizes, start, genotypes.reshape(genotypes.shape[1:]))
+    return pl.pallas_call(hand_out, out_shape=shapes)(*results)
 
 
 def solution(mesh):

time: 132 us -> 126 us (0.955)
  local copies, waits for them, and re-layouts: 3.04 us -> 0 us
  Pallas kernels: 127 us -> 124 us
    pallas_call x1 -> x2, Pallas kernels: 127 us -> 124 us  [the longest x1 122 us: body(): pl.pallas_call(kernel, out_shape=shapes, in_specs=[pl.BlockSpec(memory_sp...]
    unnamed x2 -> x0, local copies, waits for them, and re-layouts: 3.04 us -> none
where the time goes in v3:
time: 126 us; the launch traced here: 125 us
  Pallas kernels  124 us (98%)
  between operations  1.28 us (1%)
    pallas_call x1, Pallas kernels, body(): pl.pallas_call(kernel, out_shape=shapes, in_specs=[pl.BlockSpec(memory_sp...  122 us

profile of v3, /device:TPU:1, one launch (start us, length us, event | category | flops | bytes accessed | tf_op | source)
XLA Modules:
  0.0 125.4 jit_solution(5782457320356469206)
XLA Ops:
  1.3 122.4 %shard_map.50 = (f32[1,32,256]{2,1,0:T(8,128)}, f32[1,256,256]{2,1,0:T(8,128)}) custom-call(s32[1]{0:T(128)S(6)} %copy.5.sizes, f32[1,32,256]{2,1,0:T(8,128)} %start.1, bf16[1024,2048]{1,0:T(8,128)(2,1)} %bitcast.1), custom_call_target="tpu_custom_call" | custom-call | tf_op jit(solution)/shard_map/pallas_call | solution.py:411
  123.7 1.7 %shard_map.51 = (f32[1,32,256]{2,1,0:T(8,128)}, f32[1,256,256]{2,1,0:T(8,128)}) custom-call(f32[1,32,256]{2,1,0:T(8,128)} %get-tuple-element.4.basis, f32[1,256,256]{2,1,0:T(8,128)} %get-tuple-element.5.scaled), custom_call_target="tpu_custom_call" | custom-call | tf_op jit(solution)/shard_map/pallas_call | solution.py:450

commit v4 on v3

--- a/solution.py
+++ b/solution.py
@@ -147,7 +147,7 @@
 
 
 def kernel(sizes, start, x_hbm, basis, scaled, x, xt, gath, y, part, sum1, got1, got2, aug,
-           mine, mgot1, mgot2, mgot3, mall, tbuf, xsem, gs, gr, ls, lr, ms, mr, ts, tr):
+           mine, mgot1, mgot2, mgot3, mall, tbuf, xsem, gs, gr, hs, hr, ls, lr, ks, kr, ms, mr, ts, tr):
     blk = lax.axis_index("blk")
     smp = lax.axis_index("smp")
     at = [smp // 16, lax.rem(smp // 4, 4), lax.rem(smp, 4)]
@@ -179,16 +179,15 @@
     pl.semaphore_wait(barrier, len(steps) + 1)
 
     def copies(src, dst, send, recv, axis, ds=(1, 2, 3)):
-        out = []
         for d in ds:
             pos = lax.rem(at[axis] + d, 4)
-            c = pltpu.make_async_remote_copy(
-                src_ref=src(pos), dst_ref=dst(d), send_sem=send.at[d - 1], recv_sem=recv.at[d - 1],
+            pltpu.make_async_remote_copy(
+                src_ref=src(pos), dst_ref=dst(d), send_sem=send, recv_sem=recv,
                 device_id=peer(axis, pos), device_id_type=MESH,
-            )
-            c.start()
-            out.append(c)
-        return out
+            ).start()
+
+    def drain(sem, like):
+        pltpu.make_async_copy(like, like, sem).wait()
 
     def pick(axis_index, n, pos):
         return tuple(pos if i == axis_index else slice(None) for i in range(n))
@@ -203,39 +202,33 @@
         where = list(at)
         where[u] = lax.rem(at[u] + du, 4)
         where[v] = lax.rem(at[v] + dv, 4)
-        k = pltpu.make_async_remote_copy(
-            src_ref=src, dst_ref=dst, send_sem=send.at[4 * du + dv - 1], recv_sem=recv.at[4 * du + dv - 1],
+        pltpu.make_async_remote_copy(
+            src_ref=src, dst_ref=dst, send_sem=send, recv_sem=recv,
             device_id=(blk, where[0] * 16 + where[1] * 4 + where[2]), device_id_type=MESH,
-        )
-        k.start()
-        return k
-
-    def wait_all(running):
-        for cs in running:
-            for k in cs:
-                k.wait()
+        ).start()
 
     def gather(phase):
         buf = gath.at[phase % 2]
-        short, long = {}, []
         for du in (0, 1, 3, 2):
             for c in range(3):
                 view = buf.at[at[0], at[1], at[2], pl.ds(*GATHER_ROWS[c])]
                 for dv in range(4):
                     if du + dv:
-                        short[c, du, dv] = plane_copy(c, du, dv, view, view, gs.at[phase, c], gr.at[phase, c])
+                        plane_copy(c, du, dv, view, view, gs.at[c, min(du, 1)], gr.at[c, du])
         yield
         for du in (0, 1, 3, 2):
             for c in range(3):
-                for dv in range(4):
-                    if du + dv:
-                        short[c, du, dv].wait_recv()
+                rows = pl.ds(*GATHER_ROWS[c])
+                drain(gr.at[c, du], buf.at[0, 0, 0 : 4 if du else 3, rows])
                 line = lax.rem(at[OTHERS[c][0]] + 4 - du, 4)
-                view = buf.at[place(c, at[c], line, (pl.ds(*GATHER_ROWS[c]),))]
-                long.append(copies(lambda pos: view, lambda d: view, ls.at[phase, c, du], lr.at[phase, c, du], c))
-        for k in short.values():
-            k.wait_send()
-        wait_all(long)
+                view = buf.at[place(c, at[c], line, (rows,))]
+                copies(lambda pos: view, lambda d: view, hs.at[c], hr.at[c], c)
+        for c in range(3):
+            rows = pl.ds(*GATHER_ROWS[c])
+            drain(gs.at[c, 0], buf.at[0, 0, 0:3, rows])
+            drain(gs.at[c, 1], buf.at[0, 0:3, :, rows])
+            drain(hs.at[c], buf.at[0:3, :, :, rows])
+            drain(hr.at[c], buf.at[0:3, :, :, rows])
 
     def halves(buf):
         full = buf[...]
@@ -262,14 +255,12 @@
             part[z, pl.ds(2 * m, 2), :, 32:64, :] = t[:, 128:].reshape(2, 4, 32, 128)
 
     def scatter(phase, result):
-        long, short = {(0, du): [] for du in range(4)}, {}
-
         def send(c, du, d):
             rows = (pl.ds(*SUM_ROWS[c]),)
             line = lax.rem(at[OTHERS[c][0]] + du, 4)
-            long.setdefault((c, du), []).extend(copies(
+            copies(
                 lambda pos: part.at[place(c, pos, line, rows)], lambda d: got1.at[(d - 1, du, slice(None)) + rows],
-                ls.at[3 + phase, c, du], lr.at[3 + phase, c, du], c, d))
+                ls.at[c], lr.at[c, du], c, d)
 
         for du in (2, 1, 3, 0):
             expand(lax.rem(at[0] + du, 4))
@@ -282,8 +273,7 @@
         for du in (2, 1, 3, 0):
             for c in range(3):
                 r0, n = SUM_ROWS[c]
-                for k in long[c, du]:
-                    k.wait_recv()
+                drain(lr.at[c, du], got1.at[:, du, :, pl.ds(r0, n)])
                 line = lax.rem(at[OTHERS[c][0]] + du, 4)
                 v = part[place(c, at[c], line, (slice(r0, r0 + n),))]
                 for d in range(3):
@@ -292,21 +282,19 @@
                 for dv in range(4):
                     if du + dv:
                         pv = lax.rem(at[OTHERS[c][1]] + dv, 4)
-                        short[c, du, dv] = plane_copy(
+                        plane_copy(
                             c, du, dv, sum1.at[du, pv, pl.ds(r0, n)], got2.at[4 * du + dv - 1, pl.ds(r0, n)],
-                            gs.at[3 + phase, c], gr.at[3 + phase, c])
+                            ks.at[c], kr.at[c])
             yield
-        for k in [k for ks in long.values() for k in ks]:
-            k.wait_send()
         pieces = []
         for c in range(3):
             r0, n = SUM_ROWS[c]
+            drain(ls.at[c], got1.at[:, :, :, pl.ds(r0, n)])
+            drain(ks.at[c], got2.at[:, pl.ds(r0, n)])
+            drain(kr.at[c], got2.at[:, pl.ds(r0, n)])
             v = sum1[0, at[OTHERS[c][1]], r0 : r0 + n, :]
-            for du in (2, 1, 3, 0):
-                for dv in range(4):
-                    if du + dv:
-                        short[c, du, dv].wait()
-                        v = v + got2[4 * du + dv - 1, r0 : r0 + n, :]
+            for i in range(15):
+                v = v + got2[i, r0 : r0 + n, :]
             pieces.append(v)
         v = jnp.concatenate(pieces, axis=0)
         v = jnp.concatenate([v[:32], v[32:]], axis=1)
@@ -362,14 +350,14 @@
     total = (first[:, 0:256] + (cross + cross.T) + last) * (1.0 / (64 * 1024))
     for c, (r, q) in enumerate(((0, 0), (0, 128), (128, 128))):
         mine[c] = total[r : r + 128, q : q + 128].reshape(4, 32, 128)
-    running = [copies(lambda pos: mine.at[c, pos], lambda d: mgot1.at[c, d - 1], ms.at[c, 0], mr.at[c, 0], o[0]) for c, o in enumerate(ORDERS)]
+    for c, o in enumerate(ORDERS):
+        copies(lambda pos: mine.at[c, pos], lambda d: mgot1.at[c, d - 1], ms.at[c, 0], mr.at[c, 0], o[0])
     factor_start(aug, square(0))
     factor_part(aug, 0, 4)
     for stage, (had, now) in ((1, (None, mgot2)), (2, (mgot2, mgot3)), (3, (mgot3, mall))):
-        after = []
         for c, o in enumerate(ORDERS):
-            for k in running[c]:
-                k.wait()
+            drain(mr.at[c, stage - 1], mgot1.at[c])
+            drain(ms.at[c, stage - 1], mgot1.at[c])
             if stage == 1:
                 v = mine[c, at[o[0]]] + mgot1[c, 0] + mgot1[c, 1] + mgot1[c, 2]
             else:
@@ -377,14 +365,13 @@
             axis = o[stage] if stage < 3 else o[0]
             now[c, at[axis]] = v
             view = now.at[c, at[axis]]
-            after.append(copies(lambda pos: view, lambda d: view, ms.at[c, stage], mr.at[c, stage], axis))
-        running = after
+            copies(lambda pos: view, lambda d: view, ms.at[c, stage], mr.at[c, stage], axis)
         factor_part(aug, 4 * stage, 4)
     low = aug[:, 256:512]
     basis[0] = exact(image, low, ((1,), (1,))) * math.sqrt(CAP)
-    for cs in running:
-        for k in cs:
-            k.wait()
+    for c in range(3):
+        drain(mr.at[c, 3], mgot1.at[c])
+        drain(ms.at[c, 3], mgot1.at[c])
     b00, b01, b11 = (mall[c].reshape(128, 128) for c in range(3))
     full = jnp.concatenate([jnp.concatenate([b00, b01], axis=1), jnp.concatenate([b01.T, b11], axis=1)], axis=0)
     left = exact(low, full, ((1,), (0,)))
@@ -434,12 +421,16 @@
             vm((3, 4, 32, 128), F32),
             vm((2, 8, 128), F32),
             dma,
-            dma((5, 3, 15)),
-            dma((5, 3, 15)),
-            dma((5, 3, 4, 3)),
-            dma((5, 3, 4, 3)),
-            dma((3, 4, 3)),
-            dma((3, 4, 3)),
+            dma((3, 2)),
+            dma((3, 4)),
+            dma((3,)),
+            dma((3,)),
+            dma((3,)),
+            dma((3, 4)),
+            dma((3,)),
+            dma((3,)),
+            dma((3, 4)),
+            dma((3, 4)),
             dma,
             dma,
         ],

time: 126 us -> 118 us (0.937)
  Pallas kernels: 124 us -> 116 us
    pallas_call x1, Pallas kernels: 122 us -> 115 us  [body(): pl.pallas_call(kernel, out_shape=shapes, in_specs=[pl.BlockSpec(memory_sp...]
where the time goes in v4:
time: 118 us
  Pallas kernels  116 us (98%)
  between operations  1.28 us (1%)
    pallas_call x1, Pallas kernels, body(): pl.pallas_call(kernel, out_shape=shapes, in_specs=[pl.BlockSpec(memory_sp...  115 us

profile of v4, /device:TPU:1, one launch (start us, length us, event | category | flops | bytes accessed | tf_op | source)
XLA Modules:
  0.0 117.5 jit_solution(11475908367503486043)
XLA Ops:
  1.3 114.5 %shard_map.50 = (f32[1,32,256]{2,1,0:T(8,128)}, f32[1,256,256]{2,1,0:T(8,128)}) custom-call(s32[1]{0:T(128)S(6)} %copy.5.sizes, f32[1,32,256]{2,1,0:T(8,128)} %start.1, bf16[1024,2048]{1,0:T(8,128)(2,1)} %bitcast.1), custom_call_target="tpu_custom_call" | custom-call | tf_op jit(solution)/shard_map/pallas_call | solution.py:398
  115.8 1.7 %shard_map.51 = (f32[1,32,256]{2,1,0:T(8,128)}, f32[1,256,256]{2,1,0:T(8,128)}) custom-call(f32[1,32,256]{2,1,0:T(8,128)} %get-tuple-element.4.basis, f32[1,256,256]{2,1,0:T(8,128)} %get-tuple-element.5.scaled), custom_call_target="tpu_custom_call" | custom-call | tf_op jit(solution)/shard_map/pallas_call | solution.py:441

commit v5 on v4

--- a/solution.py
+++ b/solution.py
@@ -146,8 +146,8 @@
     return first, last
 
 
-def kernel(sizes, start, x_hbm, basis, scaled, x, xt, gath, y, part, sum1, got1, got2, aug,
-           mine, mgot1, mgot2, mgot3, mall, tbuf, xsem, gs, gr, hs, hr, ls, lr, ks, kr, ms, mr, ts, tr):
+def kernel(sizes_hbm, start_hbm, x_hbm, basis, scaled, x, xt, gath, y, part, sum1, got1, got2, aug,
+           mine, mgot1, mgot2, mgot3, mall, tbuf, sizes, start, xsem, isem, gs, gr, hs, hr, ls, lr, ks, kr, ms, mr, ts, tr):
     blk = lax.axis_index("blk")
     smp = lax.axis_index("smp")
     at = [smp // 16, lax.rem(smp // 4, 4), lax.rem(smp, 4)]
@@ -157,8 +157,10 @@
         where[axis] = pos
         return (blk, where[0] * 16 + where[1] * 4 + where[2])
 
+    small = (pltpu.make_async_copy(sizes_hbm, sizes, isem.at[0]), pltpu.make_async_copy(start_hbm, start, isem.at[1]))
     load = pltpu.make_async_copy(x_hbm, x, xsem)
-    load.start()
+    for copy in small:
+        copy.start()
     barrier = pltpu.get_barrier_semaphore()
     steps = [(dz, dy, dx) for dz in range(4) for dy in range(4) for dx in range(4) if 0 < (dz > 0) + (dy > 0) + (dx > 0) < 3]
     for step in steps:
@@ -166,6 +168,9 @@
         pl.semaphore_signal(barrier, inc=1, device_id=(blk, z * 16 + y_ * 4 + x_), device_id_type=MESH)
     pl.semaphore_signal(barrier, inc=1, device_id=(1 - blk, smp), device_id_type=MESH)
 
+    load.start()
+    for copy in small:
+        copy.wait()
     size = sizes[0]
     live = lax.broadcasted_iota(jnp.int32, (32, 256), 0) + smp * 32 < size
 
@@ -330,16 +335,9 @@
     s = scatter(1, out)
     next(s)
     factor_start(aug, square(1))
-    factor_part(aug, 0, 4)
-    next(s)
-    factor_part(aug, 4, 2)
-    next(s)
-    factor_part(aug, 6, 2)
-    next(s)
-    factor_part(aug, 8, 2)
-    next(s)
-    factor_part(aug, 10, 6)
-    run(s)
+    for first, count in ((0, 5), (5, 1), (6, 2), (8, 3), (11, 5)):
+        factor_part(aug, first, count)
+        next(s, None)
     image = exact(out[0], aug[:, 256:512], ((1,), (1,)))
     put_own(gath.at[0], image)
     run(gather(2))
@@ -353,8 +351,8 @@
     for c, o in enumerate(ORDERS):
         copies(lambda pos: mine.at[c, pos], lambda d: mgot1.at[c, d - 1], ms.at[c, 0], mr.at[c, 0], o[0])
     factor_start(aug, square(0))
-    factor_part(aug, 0, 4)
-    for stage, (had, now) in ((1, (None, mgot2)), (2, (mgot2, mgot3)), (3, (mgot3, mall))):
+    factor_part(aug, 0, 3)
+    for stage, had, now, pairs in ((1, None, mgot2, (3, 5)), (2, mgot2, mgot3, (8, 5)), (3, mgot3, mall, (13, 3))):
         for c, o in enumerate(ORDERS):
             drain(mr.at[c, stage - 1], mgot1.at[c])
             drain(ms.at[c, stage - 1], mgot1.at[c])
@@ -366,9 +364,8 @@
             now[c, at[axis]] = v
             view = now.at[c, at[axis]]
             copies(lambda pos: view, lambda d: view, ms.at[c, stage], mr.at[c, stage], axis)
-        factor_part(aug, 4 * stage, 4)
+        factor_part(aug, *pairs)
     low = aug[:, 256:512]
-    basis[0] = exact(image, low, ((1,), (1,))) * math.sqrt(CAP)
     for c in range(3):
         drain(mr.at[c, 3], mgot1.at[c])
         drain(ms.at[c, 3], mgot1.at[c])
@@ -381,6 +378,7 @@
     )
     c.start()
     ray = exact(left, low, ((1,), (1,)))
+    basis[0] = exact(image, low, ((1,), (1,))) * math.sqrt(CAP)
     c.wait()
     both = tbuf[0, 0:1, 0:1] + tbuf[1, 0:1, 0:1]
     scaled[0] = ray * (2.0 * K) / both
@@ -399,8 +397,8 @@
         kernel,
         out_shape=shapes,
         in_specs=[
-            pl.BlockSpec(memory_space=pltpu.SMEM),
-            pl.BlockSpec(memory_space=pltpu.VMEM),
+            pl.BlockSpec(memory_space=pl.ANY),
+            pl.BlockSpec(memory_space=pl.ANY),
             pl.BlockSpec(memory_space=pl.ANY),
         ],
         out_specs=(pl.BlockSpec(memory_space=pltpu.VMEM), pl.BlockSpec(memory_space=pltpu.VMEM)),
@@ -420,7 +418,10 @@
             vm((3, 4, 32, 128), F32),
             vm((3, 4, 32, 128), F32),
             vm((2, 8, 128), F32),
+            pltpu.SMEM((1,), jnp.int32),
+            vm((1, 32, K), F32),
             dma,
+            dma((2,)),
             dma((3, 2)),
             dma((3, 4)),
             dma((3,)),

time: 118 us -> 117 us (level)
  no operation moved by 1% of the time
where the time goes in v5:
time: 117 us; the launch traced here: 116 us
  Pallas kernels  115 us (98%)
  between operations  1.28 us (1%)
    pallas_call x1, Pallas kernels, body(): pl.pallas_call(kernel, out_shape=shapes, in_specs=[pl.BlockSpec(memory_sp...  113 us

profile of v5, /device:TPU:1, one launch (start us, length us, event | category | flops | bytes accessed | tf_op | source)
XLA Modules:
  0.0 116.5 jit_solution(13003800555779711034)
XLA Ops:
  1.3 113.5 %shard_map.50 = (f32[1,32,256]{2,1,0:T(8,128)}, f32[1,256,256]{2,1,0:T(8,128)}) custom-call(s32[1]{0:T(128)S(6)} %copy.5.sizes_hbm, f32[1,32,256]{2,1,0:T(8,128)} %start_hbm.1, bf16[1024,2048]{1,0:T(8,128)(2,1)} %bitcast.1), custom_call_target="tpu_custom_call" | custom-call | tf_op jit(solution)/shard_map/pallas_call | solution.py:396
  114.8 1.7 %shard_map.51 = (f32[1,32,256]{2,1,0:T(8,128)}, f32[1,256,256]{2,1,0:T(8,128)}) custom-call(f32[1,32,256]{2,1,0:T(8,128)} %get-tuple-element.4.basis, f32[1,256,256]{2,1,0:T(8,128)} %get-tuple-element.5.scaled), custom_call_target="tpu_custom_call" | custom-call | tf_op jit(solution)/shard_map/pallas_call | solution.py:442

commit v6 on v5

--- a/solution.py
+++ b/solution.py
@@ -15,8 +15,8 @@
 MESH = pl.DeviceIdType.MESH
 OTHERS = ((1, 2), (0, 2), (0, 1))
 ORDERS = ((0, 1, 2), (1, 2, 0), (2, 0, 1))
-SUM_ROWS = ((0, 24), (24, 24), (48, 16))
-GATHER_ROWS = ((0, 48), (48, 48), (96, 32))
+SUM_ROWS = ((0, 16), (16, 24), (40, 24))
+GATHER_ROWS = ((0, 32), (32, 48), (80, 48))
 
 
 def split3(v):

time: 117 us -> 112 us (0.957)
  Pallas kernels: 115 us -> 111 us
    pallas_call x1, Pallas kernels: 113 us -> 109 us  [body(): pl.pallas_call(kernel, out_shape=shapes, in_specs=[pl.BlockSpec(memory_sp...]
where the time goes in v6:
time: 112 us
  Pallas kernels  111 us (99%)
  between operations  1.28 us (1%)
    pallas_call x1, Pallas kernels, body(): pl.pallas_call(kernel, out_shape=shapes, in_specs=[pl.BlockSpec(memory_sp...  109 us

profile of v6, /device:TPU:1, one launch (start us, length us, event | category | flops | bytes accessed | tf_op | source)
XLA Modules:
  0.0 112.3 jit_solution(7177667933269761092)
XLA Ops:
  1.3 109.3 %shard_map.50 = (f32[1,32,256]{2,1,0:T(8,128)}, f32[1,256,256]{2,1,0:T(8,128)}) custom-call(s32[1]{0:T(128)S(6)} %copy.5.sizes_hbm, f32[1,32,256]{2,1,0:T(8,128)} %start_hbm.1, bf16[1024,2048]{1,0:T(8,128)(2,1)} %bitcast.1), custom_call_target="tpu_custom_call" | custom-call | tf_op jit(solution)/shard_map/pallas_call | solution.py:396
  110.6 1.7 %shard_map.51 = (f32[1,32,256]{2,1,0:T(8,128)}, f32[1,256,256]{2,1,0:T(8,128)}) custom-call(f32[1,32,256]{2,1,0:T(8,128)} %get-tuple-element.4.basis, f32[1,256,256]{2,1,0:T(8,128)} %get-tuple-element.5.scaled), custom_call_target="tpu_custom_call" | custom-call | tf_op jit(solution)/shard_map/pallas_call | solution.py:442
